TPU v7x, 512 devices: a whole 4x4x16 slice. The times are simulated.
512 devices in a mesh: space: 16 (over y, x_hi, core), date: 32 (over x_lo, z).
Axes of the slice: x: 4 (x_hi: 2, x_lo: 2; x = x_hi * 2 + x_lo), y: 4, z: 16, core: 2. Of those that a mesh axis runs over, the one named last changes fastest.
Arguments:
- obs: bfloat16 [7, 768, 128, 512], P(None, 'date', 'space'), may hold values from -30 to 30
- valid: int32 [768, 128, 512], P('date', 'space'), may hold values from 0 to 1
- days: int32 [768], P('date'), may hold values from 0 to 3649, as said below
Outputs:
- coefficients: float32 [7, 8, 128, 512], P(None, None, 'space', 'date')
- noise_scale: float32 [128, 512], P('space', 'date')
Inputs may be any that keep to these rules, and one draw needn't show every extreme that they name: `days`: day numbers of the acquisitions, in no particular order.
All inputs are finite; a program needn't handle non-finite values.
Results may differ from a plain program's by a relative error of at most 0.0003.
Values may be sent and summed in bfloat16 or wider, within the bound.
A program may use at most 128 MiB of HBM per device.

v0:
```python
import math
import jax
import jax.numpy as jnp
import numpy as np
from jax import lax
from jax.sharding import PartitionSpec as P

ITERS = 2
tukey_const = 4.685
ridge_value = 1.0
scale_eps = 1e-06
highest = lax.Precision.HIGHEST
pair_first = np.array(
    [row_index for row_index in range(8) for col_index in range(row_index, 8)], dtype=np.int32
)
pair_second = np.array(
    [col_index for row_index in range(8) for col_index in range(row_index, 8)], dtype=np.int32
)


def padded_2(block, sides, width):
    for axis, dim in sides:
        count = lax.axis_size(axis)
        forward = [(i, i + 1) for i in range(count - 1)]
        backward = [(target, source) for source, target in forward]
        low = lax.ppermute(
            lax.slice_in_dim(block, block.shape[dim] - width, None, axis=dim), axis, forward
        )
        high = lax.ppermute(lax.slice_in_dim(block, 0, width, axis=dim), axis, backward)
        block = jnp.concatenate([low, block, high], axis=dim)
    return block


def design(day_numbers):
    day_float = day_numbers.astype(jnp.float32)
    columns = [jnp.ones_like(day_float), (day_float - 1825.0) / 1825.0]
    angle = day_float * (2.0 * math.pi / 365.25)
    for harmonic in range(1, 4):
        columns.append(jnp.cos(harmonic * angle))
        columns.append(jnp.sin(harmonic * angle))
    return jnp.stack(columns, axis=1)


def form_moments(design_rows, weighted, observed):
    products = design_rows[:, pair_first] * design_rows[:, pair_second]
    gram_terms = jnp.dot(
        products.T, weighted, precision=highest, preferred_element_type=jnp.float32
    )
    cross_terms = jnp.einsum(
        "dk,bdp->bkp",
        design_rows,
        weighted[None] * observed,
        precision=highest,
        preferred_element_type=jnp.float32,
    )
    return jnp.concatenate([gram_terms, cross_terms.reshape(-1, weighted.shape[1])], axis=0)


def solve_terms(summed, band_count):
    term_count = 8
    entries = {}
    position = 0
    for row_index in range(term_count):
        for col_index in range(row_index, term_count):
            entries[row_index, col_index] = summed[position]
            position += 1
    right_sides = summed[position:].reshape((band_count, term_count) + summed.shape[1:])
    lower_factor = {}
    for col_index in range(term_count):
        pivot_value = entries[col_index, col_index] + ridge_value
        for inner_index in range(col_index):
            pivot_value = (
                pivot_value
                - lower_factor[col_index, inner_index] * lower_factor[col_index, inner_index]
            )
        pivot_root = jnp.sqrt(pivot_value)
        lower_factor[col_index, col_index] = pivot_root
        for row_index in range(col_index + 1, term_count):
            entry_value = entries[col_index, row_index]
            for inner_index in range(col_index):
                entry_value = (
                    entry_value
                    - lower_factor[row_index, inner_index] * lower_factor[col_index, inner_index]
                )
            lower_factor[row_index, col_index] = entry_value / pivot_root
    forward = []
    for row_index in range(term_count):
        running = right_sides[:, row_index]
        for inner_index in range(row_index):
            running = running - lower_factor[row_index, inner_index][None] * forward[inner_index]
        forward.append(running / lower_factor[row_index, row_index][None])
    solved = [None] * term_count
    for row_index in reversed(range(term_count)):
        running = forward[row_index]
        for inner_index in range(row_index + 1, term_count):
            running = running - lower_factor[inner_index, row_index][None] * solved[inner_index]
        solved[row_index] = running / lower_factor[row_index, row_index][None]
    return (jnp.stack(solved, axis=1), entries[0, 0])


def residual_power(design_rows, observed, coefficient):
    fitted = jnp.einsum(
        "dk,bkp->bdp",
        design_rows,
        coefficient,
        precision=highest,
        preferred_element_type=jnp.float32,
    )
    misfit = observed - fitted
    return jnp.mean(misfit * misfit, axis=0)


def box_sum(padded, row_count, col_count):
    across = padded[0:row_count]
    for offset in range(1, 5):
        across = across + padded[offset : offset + row_count]
    window_sum = across[:, 0:col_count]
    for offset in range(1, 5):
        window_sum = window_sum + across[:, offset : offset + col_count]
    return window_sum


def window_counts(first_index, length, whole):
    global_index = first_index + jnp.arange(length, dtype=jnp.int32)
    return (jnp.minimum(global_index + 2, whole - 1) - jnp.maximum(global_index - 2, 0) + 1).astype(
        jnp.float32
    )


def spread_rows(spread, weight_total, row_count, col_count):
    full_spread = lax.psum(spread, "date")
    variance = full_spread / (1.0 + weight_total)
    padded = padded_2(variance.reshape(row_count, col_count), (("space", 0),), 2)
    return jnp.pad(padded, ((0, 0), (2, 2)))


def next_weight(resid_power, smooth, mask_float):
    scaled = jnp.minimum(
        resid_power / (tukey_const * tukey_const * (smooth[None] + scale_eps)), 1.0
    )
    return mask_float * (1.0 - scaled) * (1.0 - scaled)


def on_device(obs, valid, days):
    band_count, date_count, row_count, col_count = obs.shape
    date_devices = lax.axis_size("date")
    date_index = lax.axis_index("date")
    cols_local = col_count // date_devices
    row_first = lax.axis_index("space") * row_count
    grid_rows = row_count * lax.axis_size("space")
    pixels = row_count * col_count
    mask_float = valid.astype(jnp.float32).reshape(date_count, pixels)
    observed = obs.astype(jnp.float32).reshape(band_count, date_count, pixels)
    design_rows = design(days)
    col_first = 0
    slice_start = date_index * cols_local
    counts = (
        window_counts(row_first, row_count, grid_rows)[:, None]
        * window_counts(col_first, col_count, col_count)[None, :]
    )
    weighted = mask_float
    for step in range(ITERS):
        local_terms = form_moments(design_rows, weighted, observed)
        summed = lax.psum(local_terms, "date")
        coefficient, weight_total = solve_terms(summed, band_count)
        resid_power = residual_power(design_rows, observed, coefficient)
        spread = jnp.sum(weighted * resid_power, axis=0)
        padded = spread_rows(spread, weight_total, row_count, col_count)
        smooth = (box_sum(padded, row_count, col_count) / counts).reshape(pixels)
        if step + 1 < ITERS:
            weighted = next_weight(resid_power, smooth, mask_float)
    coefficient = coefficient.reshape(band_count, 8, row_count, col_count)
    noise_scale = jnp.sqrt(smooth + scale_eps).reshape(row_count, col_count)
    coefficients = lax.dynamic_slice_in_dim(coefficient, slice_start, cols_local, 3)
    noise_block = lax.dynamic_slice_in_dim(noise_scale, slice_start, cols_local, 1)
    return (coefficients, noise_block)


def solution(mesh):
    in_specs = (P(None, "date", "space", None), P("date", "space", None), P("date"))
    out_specs = (P(None, None, "space", "date"), P("space", "date"))
    return jax.shard_map(
        on_device, mesh=mesh, in_specs=in_specs, out_specs=out_specs, check_vma=False
    )
```

profile of v0, /device:TPU:1, one launch (start us, length us, event | category | flops | bytes accessed | tf_op | source)
XLA Modules:
  0.0 877.3 jit_solution(6437620720839090686)
XLA Ops:
  11.1 2.4 reshape.5086
  14.7 1.6 convolution_bitcast_fusion.3
  17.9 245.5 %all-reduce.5.cloned.1.call-done = f32[92,4096]{1,0:T(8,128)} async-done(((f32[92,4096]{1,0:T(8,128)}), f32[92,4096]{1,0:T(8,128)}) %all-reduce.5.cloned.1.call-update) | async-done | bytes 1507344 | tf_op jit(solution)/shard_map/psum | solution.py:164
  263.4 2.4 slice_add_fusion.28
  265.7 1.8 subtract_sqrt_fusion.11
  267.6 1.7 subtract_sqrt_fusion.10
  269.3 1.6 rsqrt_multiply_fusion.9
  272.4 2.0 subtract_divide_fusion.19
  274.4 3.7 subtract_divide_fusion.11
  278.1 3.7 stack.72
  281.8 3.8 fusion.6
  287.9 93.7 %psum.29 = f32[4096]{0:T(1024)} all-reduce(f32[4096]{0:T(1024)} %bitcast.399), channel_id=1, replica_groups=mesh['space'=16,'date'=32] {'date'}, use_global_device_ids=true, to_apply=%region_3.0 | all-reduce | flops 4096 | bytes 32768 | tf_op jit(solution)/shard_map/psum | solution.py:131
  383.6 54.4 %collective-permute-start = (f32[2,512]{1,0:T(2,128)}, f32[2,512]{1,0:T(2,128)S(1)}, u32[]{:S(2)}, u32[]{:S(2)}) collective-permute-start(f32[2,512]{1,0:T(2,128)} %slice.432), channel_id=1, source_target_pairs={{0,32},{32,64},{64,96},{96,128},{128,160},{160,192},{192,224},{224... | collective-permute-start | bytes 12296 | tf_op jit(solution)/shard_map/ppermute | solution.py:26
  438.5 2.1 collective-permute-start.1
  442.5 2.6 collective-permute-done.1
  448.0 1.6 convolution_bitcast_fusion.2
  451.6 231.3 %all-reduce.7.cloned.1.call-done = f32[92,4096]{1,0:T(8,128)} async-done(((f32[92,4096]{1,0:T(8,128)}), f32[92,4096]{1,0:T(8,128)}) %all-reduce.7.cloned.1.call-update) | async-done | bytes 1507344 | tf_op jit(solution)/shard_map/psum | solution.py:164
  682.9 1.8 slice_add_fusion.16
  684.7 1.9 subtract_sqrt_fusion.5
  686.5 1.7 subtract_sqrt_fusion.4
  688.3 1.6 rsqrt_multiply_fusion.6
  691.3 3.8 fusion.144
  698.5 1.4 fusion.151
  699.9 1.5 fusion.152
  701.3 1.6 fusion.153
  703.6 2.1 fusion.154
  705.7 3.6 stack.82
  709.3 3.8 fusion.7
  714.4 93.7 %psum.31 = f32[4096]{0:T(1024)S(1)} all-reduce(f32[4096]{0:T(1024)S(1)} %bitcast.400), channel_id=1, replica_groups=mesh['space'=16,'date'=32] {'date'}, use_global_device_ids=true, to_apply=%region_7.8 | all-reduce | flops 4096 | bytes 32768 | tf_op jit(solution)/shard_map/psum | solution.py:131
  808.1 54.4 %collective-permute-start.2 = (f32[2,512]{1,0:T(2,128)S(1)}, f32[2,512]{1,0:T(2,128)S(1)}, u32[]{:S(2)}, u32[]{:S(2)}) collective-permute-start(f32[2,512]{1,0:T(2,128)S(1)} %slice.491), channel_id=1, source_target_pairs={{0,32},{32,64},{64,96},{96,128},{128,160},{160,192},{192,224},{224... | collective-permute-start | bytes 12296 | tf_op jit(solution)/shard_map/ppermute | solution.py:26
  862.5 1.9 collective-permute-start.3
  865.9 3.0 collective-permute-done.3
  (116 shorter events, 29.2 us)
Async XLA Ops:
  7.2 256.2 %all-reduce.5.cloned.1.call-start = ((), (), s32[]{:S(2)}) async-start(), calls=%async_computation | async-start | bytes 3145728 | tf_op jit(solution)/shard_map/psum | solution.py:164
  13.5 0.6 copy-start.15
  17.6 665.3 %all-reduce.7.cloned.1.call-start = ((), (), s32[]{:S(2)}) async-start(), calls=%async_computation.1 | async-start | bytes 3145728 | tf_op jit(solution)/shard_map/psum | solution.py:164
  263.4 7.5 copy-start.5
  285.6 1.0 copy-start
  286.6 0.8 copy-start.2
  382.4 0.6 copy-start.19
  383.6 59.0 %collective-permute-start = (f32[2,512]{1,0:T(2,128)}, f32[2,512]{1,0:T(2,128)S(1)}, u32[]{:S(2)}, u32[]{:S(2)}) collective-permute-start(f32[2,512]{1,0:T(2,128)} %slice.432), channel_id=1, source_target_pairs={{0,32},{32,64},{64,96},{96,128},{128,160},{160,192},{192,224},{224... | collective-permute-start | bytes 12296 | tf_op jit(solution)/shard_map/ppermute | solution.py:26
  438.5 6.6 collective-permute-start.1
  447.3 0.6 copy-start.17
  448.0 1.6 copy-start.16
  682.9 7.0 copy-start.4
  702.9 0.6 copy-start.6
  713.1 1.0 copy-start.1
  713.1 1.1 copy-start.3
  713.1 1.1 copy-start.18
  713.1 151.3 %copy-start.11 = (f32[7,4096]{1,0:T(8,128)S(1)}, f32[7,4096]{1,0:T(8,128)}, u32[]{:S(2)}) copy-start(f32[7,4096]{1,0:T(8,128)} %get-tuple-element.23) | copy-start | bytes 344068
  713.1 151.4 %copy-start.10 = (f32[7,4096]{1,0:T(8,128)S(1)}, f32[7,4096]{1,0:T(8,128)}, u32[]{:S(2)}) copy-start(f32[7,4096]{1,0:T(8,128)} %get-tuple-element.21) | copy-start | bytes 344068
  713.1 151.4 %copy-start.14 = (f32[7,4096]{1,0:T(8,128)S(1)}, f32[7,4096]{1,0:T(8,128)}, u32[]{:S(2)}) copy-start(f32[7,4096]{1,0:T(8,128)} %get-tuple-element.19) | copy-start | bytes 344068
  713.2 151.5 %copy-start.9 = (f32[7,4096]{1,0:T(8,128)S(1)}, f32[7,4096]{1,0:T(8,128)}, u32[]{:S(2)}) copy-start(f32[7,4096]{1,0:T(8,128)} %get-tuple-element.17) | copy-start | bytes 344068
  713.2 151.5 %copy-start.13 = (f32[7,4096]{1,0:T(8,128)S(1)}, f32[7,4096]{1,0:T(8,128)}, u32[]{:S(2)}) copy-start(f32[7,4096]{1,0:T(8,128)} %get-tuple-element.15) | copy-start | bytes 344068
  713.2 151.6 %copy-start.8 = (f32[7,4096]{1,0:T(8,128)S(1)}, f32[7,4096]{1,0:T(8,128)}, u32[]{:S(2)}) copy-start(f32[7,4096]{1,0:T(8,128)} %get-tuple-element.13) | copy-start | bytes 344068
  714.2 150.7 %copy-start.12 = (f32[7,4096]{1,0:T(8,128)S(1)}, f32[7,4096]{1,0:T(8,128)}, u32[]{:S(2)}) copy-start(f32[7,4096]{1,0:T(8,128)} %get-tuple-element.11) | copy-start | bytes 344068
  714.2 150.8 %copy-start.7 = (f32[7,4096]{1,0:T(8,128)S(1)}, f32[7,4096]{1,0:T(8,128)}, u32[]{:S(2)}) copy-start(f32[7,4096]{1,0:T(8,128)} %get-tuple-element.2) | copy-start | bytes 344068
  808.1 57.9 %collective-permute-start.2 = (f32[2,512]{1,0:T(2,128)S(1)}, f32[2,512]{1,0:T(2,128)S(1)}, u32[]{:S(2)}, u32[]{:S(2)}) collective-permute-start(f32[2,512]{1,0:T(2,128)S(1)} %slice.491), channel_id=1, source_target_pairs={{0,32},{32,64},{64,96},{96,128},{128,160},{160,192},{192,224},{224... | collective-permute-start | bytes 12296 | tf_op jit(solution)/shard_map/ppermute | solution.py:26
  862.5 6.4 collective-permute-start.3
Sparse Core Ops, SparseCore 0:
  17.7 245.5 all-reduce.4
  451.7 231.1 all-reduce.6
where the time goes:
time: 879 us; the launch traced here: 877 us
  waiting for transfers between devices  482 us (55%)
  blocking collectives  187 us (21%)
  starting transfers between devices  113 us (13%)
  other arithmetic  46.9 us (5%)
  local copies, waits for them, and re-layouts  20.9 us (2%)
  between operations  14.6 us (2%)
  matrix products  12 us (1%)
    psum x2, waiting for transfers between devices, on_device(): summed = lax.psum(local_terms, 'date')  477 us
    psum x2, blocking collectives, spread_rows(): full_spread = lax.psum(spread, 'date')  187 us
    ppermute x2, starting transfers between devices, padded_2(): lax.ppermute(lax.slice_in_dim(block, block.shape[dim] - width, None, axis...  109 us
  transfers between devices with their start and end apart: 6, of which 4 were waited for; matrix products, arithmetic and copies ran while one was open for 0% of the time, Pallas kernels for 0%

commit v1 on v0

--- a/solution.py
+++ b/solution.py
@@ -16,6 +16,10 @@
 pair_second = np.array(
     [col_index for row_index in range(8) for col_index in range(row_index, 8)], dtype=np.int32
 )
+
+
+def block_bind(shard_in):
+    return lax.all_gather(shard_in, axis_name="date").sum(axis=0)
 
 
 def padded_2(block, sides, width):
@@ -161,7 +165,7 @@
     weighted = mask_float
     for step in range(ITERS):
         local_terms = form_moments(design_rows, weighted, observed)
-        summed = lax.psum(local_terms, "date")
+        summed = block_bind(local_terms)
         coefficient, weight_total = solve_terms(summed, band_count)
         resid_power = residual_power(design_rows, observed, coefficient)
         spread = jnp.sum(weighted * resid_power, axis=0)

time: 879 us -> 1480 us (1.68)
  waiting for transfers between devices: 482 us -> 1090 us
  other arithmetic: 46.9 us -> 91 us
  starting transfers between devices: 113 us -> 70.2 us
    all_gather x0 -> x2, waiting for transfers between devices: none -> 1090 us  [block_bind(): return lax.all_gather(shard_in, axis_name='date').sum(axis=0)]
    psum x2 -> x0, waiting for transfers between devices: 477 us -> none  [on_device(): summed = lax.psum(local_terms, 'date')]
    ppermute x2, starting transfers between devices: 109 us -> 8.64 us  [padded_2(): lax.ppermute(lax.slice_in_dim(block, block.shape[dim] - width, None, axis...]
    ppermute x2, starting transfers between devices: 4.05 us -> 61.3 us  [padded_2(): lax.ppermute(lax.slice_in_dim(block, 0, width, axis=dim), axis, backward)]
    reduce_sum x0 -> x2, other arithmetic: none -> 37.3 us  [block_bind(): return lax.all_gather(shard_in, axis_name='date').sum(axis=0)]
  transfers between devices with their start and end apart: 6 -> 6, of which waited for: 4 -> 2; matrix products, arithmetic and copies ran while one was open for 0% -> 0% of each run, Pallas kernels for 0% -> 0%
where the time goes in v1:
time: 1480 us
  waiting for transfers between devices  1090 us (74%)
  blocking collectives  183 us (12%)
  other arithmetic  91 us (6%)
  starting transfers between devices  70.2 us (5%)
  local copies, waits for them, and re-layouts  23.2 us (2%)
    all_gather x2, waiting for transfers between devices, block_bind(): return lax.all_gather(shard_in, axis_name='date').sum(axis=0)  1090 us
    psum x2, blocking collectives, spread_rows(): full_spread = lax.psum(spread, 'date')  183 us
    ppermute x2, starting transfers between devices, padded_2(): lax.ppermute(lax.slice_in_dim(block, 0, width, axis=dim), axis, backward)  61.3 us
    reduce_sum x2, other arithmetic, block_bind(): return lax.all_gather(shard_in, axis_name='date').sum(axis=0)  37.3 us
  transfers between devices with their start and end apart: 6, of which 2 were waited for; matrix products, arithmetic and copies ran while one was open for 0% of the time, Pallas kernels for 0%

profile of v1, /device:TPU:1, one launch (start us, length us, event | category | flops | bytes accessed | tf_op | source)
XLA Modules:
  0.0 1482.3 jit_solution(3241520964354738920)
XLA Ops:
  11.1 2.4 reshape.5086
  17.9 550.6 %all-gather.7.cloned.1.call-done = f32[32,92,4096]{2,1,0:T(8,128)} async-done(((f32[1,92,4096]{2,1,0:T(8,128)}), f32[32,92,4096]{2,1,0:T(8,128)}) %all-gather.7.cloned.1.call-update) | async-done | bytes 48234512 | tf_op jit(solution)/shard_map/all_gather | solution.py:22
  568.5 18.6 %reduce_sum.58 = f32[92,4096]{1,0:T(8,128)} reduce(f32[32,92,4096]{2,1,0:T(8,128)} %all-gather.7.cloned.1.call-done, f32[]{:T(128)} %constant.16.clone.1), dimensions={0}, to_apply=%region_0.0 | reduce | flops 11681792 | bytes 49741828 | tf_op jit(solution)/shard_map/reduce_sum | solution.py:22
  587.1 2.4 slice_add_fusion.28
  590.8 1.7 subtract_sqrt_fusion.11
  592.5 1.7 subtract_sqrt_fusion.10
  594.2 1.6 rsqrt_multiply_fusion.9
  595.8 1.8 rsqrt_multiply_fusion.4
  598.7 1.8 sqrt_multiply_fusion.1
  600.8 2.0 subtract_divide_fusion.19
  602.8 3.7 subtract_divide_fusion.11
  606.5 3.6 stack.72
  610.1 3.8 fusion.6
  616.3 91.7 %psum.14 = f32[4096]{0:T(1024)} all-reduce(f32[4096]{0:T(1024)} %bitcast.403), channel_id=1, replica_groups=mesh['space'=16,'date'=32] {'date'}, use_global_device_ids=true, to_apply=%region_3.0 | all-reduce | flops 4096 | bytes 32768 | tf_op jit(solution)/shard_map/psum | solution.py:135
  710.6 30.7 %collective-permute-start.1 = (f32[2,512]{1,0:T(2,128)}, f32[2,512]{1,0:T(2,128)S(1)}, u32[]{:S(2)}, u32[]{:S(2)}) collective-permute-start(f32[2,512]{1,0:T(2,128)} %slice.434), channel_id=1, source_target_pairs={{32,0},{64,32},{96,64},{128,96},{160,128},{192,160},{224,192},{256... | collective-permute-start | bytes 12296 | tf_op jit(solution)/shard_map/ppermute | solution.py:33
  741.2 4.4 collective-permute-start
  751.8 1.6 convolution_bitcast_fusion.2
  754.7 536.5 %all-gather.9.cloned.1.call-done = f32[32,92,4096]{2,1,0:T(8,128)} async-done(((f32[1,92,4096]{2,1,0:T(8,128)}), f32[32,92,4096]{2,1,0:T(8,128)}) %all-gather.9.cloned.1.call-update) | async-done | bytes 48234512 | tf_op jit(solution)/shard_map/all_gather | solution.py:22
  1291.2 18.6 %reduce_sum.62 = f32[92,4096]{1,0:T(8,128)} reduce(f32[32,92,4096]{2,1,0:T(8,128)} %all-gather.9.cloned.1.call-done, f32[]{:T(128)} %constant.16.clone.1), dimensions={0}, to_apply=%region_4.5 | reduce | flops 11681792 | bytes 49741828 | tf_op jit(solution)/shard_map/reduce_sum | solution.py:22
  1309.9 1.8 slice_add_fusion.16
  1313.0 1.7 subtract_sqrt_fusion.5
  1314.7 1.7 subtract_sqrt_fusion.4
  1316.4 1.6 rsqrt_multiply_fusion.6
  1318.0 1.8 rsqrt_multiply_fusion.2
  1320.9 1.8 sqrt_multiply_fusion
  1323.0 3.5 fusion.144
  1335.0 2.1 fusion.154
  1337.1 3.5 stack.82
  1340.7 3.7 fusion.7
  1345.7 91.7 %psum.15 = f32[4096]{0:T(1024)S(1)} all-reduce(f32[4096]{0:T(1024)S(1)} %bitcast.404), channel_id=1, replica_groups=mesh['space'=16,'date'=32] {'date'}, use_global_device_ids=true, to_apply=%region_7.8 | all-reduce | flops 4096 | bytes 32768 | tf_op jit(solution)/shard_map/psum | solution.py:135
  1437.5 30.7 %collective-permute-start.3 = (f32[2,512]{1,0:T(2,128)S(1)}, f32[2,512]{1,0:T(2,128)S(1)}, u32[]{:S(2)}, u32[]{:S(2)}) collective-permute-start(f32[2,512]{1,0:T(2,128)S(1)} %slice.493), channel_id=1, source_target_pairs={{32,0},{64,32},{96,64},{128,96},{160,128},{192,160},{224,192},{256... | collective-permute-start | bytes 12296 | tf_op jit(solution)/shard_map/ppermute | solution.py:33
  1468.1 4.2 collective-permute-start.2
  (112 shorter events, 38.6 us)
Async XLA Ops:
  7.2 561.3 %all-gather.7.cloned.1.call-start = ((), (), s32[]{:S(2)}) async-start(), calls=%async_computation | async-start | bytes 51904512 | tf_op jit(solution)/shard_map/all_gather | solution.py:22
  13.5 0.6 copy-start.13
  17.6 1273.6 %all-gather.9.cloned.1.call-start = ((), (), s32[]{:S(2)}) async-start(), calls=%async_computation.1 | async-start | bytes 51904512 | tf_op jit(solution)/shard_map/all_gather | solution.py:22
  613.9 1.0 copy-start
  614.9 0.8 copy-start.2
  708.7 0.6 copy-start.16
  710.6 37.0 %collective-permute-start.1 = (f32[2,512]{1,0:T(2,128)}, f32[2,512]{1,0:T(2,128)S(1)}, u32[]{:S(2)}, u32[]{:S(2)}) collective-permute-start(f32[2,512]{1,0:T(2,128)} %slice.434), channel_id=1, source_target_pairs={{32,0},{64,32},{96,64},{128,96},{160,128},{192,160},{224,192},{256... | collective-permute-start | bytes 12296 | tf_op jit(solution)/shard_map/ppermute | solution.py:33
  741.2 6.4 collective-permute-start
  749.8 0.6 copy-start.14
  1334.4 0.6 copy-start.4
  1344.4 1.0 copy-start.1
  1344.4 1.1 copy-start.3
  1344.4 1.1 copy-start.15
  1344.4 127.9 %copy-start.9 = (f32[7,4096]{1,0:T(8,128)S(1)}, f32[7,4096]{1,0:T(8,128)}, u32[]{:S(2)}) copy-start(f32[7,4096]{1,0:T(8,128)} %get-tuple-element.23) | copy-start | bytes 344068
  1344.5 128.0 %copy-start.8 = (f32[7,4096]{1,0:T(8,128)S(1)}, f32[7,4096]{1,0:T(8,128)}, u32[]{:S(2)}) copy-start(f32[7,4096]{1,0:T(8,128)} %get-tuple-element.21) | copy-start | bytes 344068
  1344.5 128.1 %copy-start.12 = (f32[7,4096]{1,0:T(8,128)S(1)}, f32[7,4096]{1,0:T(8,128)}, u32[]{:S(2)}) copy-start(f32[7,4096]{1,0:T(8,128)} %get-tuple-element.19) | copy-start | bytes 344068
  1344.5 128.1 %copy-start.7 = (f32[7,4096]{1,0:T(8,128)S(1)}, f32[7,4096]{1,0:T(8,128)}, u32[]{:S(2)}) copy-start(f32[7,4096]{1,0:T(8,128)} %get-tuple-element.17) | copy-start | bytes 344068
  1344.5 128.2 %copy-start.11 = (f32[7,4096]{1,0:T(8,128)S(1)}, f32[7,4096]{1,0:T(8,128)}, u32[]{:S(2)}) copy-start(f32[7,4096]{1,0:T(8,128)} %get-tuple-element.15) | copy-start | bytes 344068
  1344.5 128.3 %copy-start.6 = (f32[7,4096]{1,0:T(8,128)S(1)}, f32[7,4096]{1,0:T(8,128)}, u32[]{:S(2)}) copy-start(f32[7,4096]{1,0:T(8,128)} %get-tuple-element.13) | copy-start | bytes 344068
  1345.5 127.3 %copy-start.10 = (f32[7,4096]{1,0:T(8,128)S(1)}, f32[7,4096]{1,0:T(8,128)}, u32[]{:S(2)}) copy-start(f32[7,4096]{1,0:T(8,128)} %get-tuple-element.11) | copy-start | bytes 344068
  1345.5 127.4 %copy-start.5 = (f32[7,4096]{1,0:T(8,128)S(1)}, f32[7,4096]{1,0:T(8,128)}, u32[]{:S(2)}) copy-start(f32[7,4096]{1,0:T(8,128)} %get-tuple-element.2) | copy-start | bytes 344068
  1437.5 36.4 %collective-permute-start.3 = (f32[2,512]{1,0:T(2,128)S(1)}, f32[2,512]{1,0:T(2,128)S(1)}, u32[]{:S(2)}, u32[]{:S(2)}) collective-permute-start(f32[2,512]{1,0:T(2,128)S(1)} %slice.493), channel_id=1, source_target_pairs={{32,0},{64,32},{96,64},{128,96},{160,128},{192,160},{224,192},{256... | collective-permute-start | bytes 12296 | tf_op jit(solution)/shard_map/ppermute | solution.py:33
  1468.1 5.8 collective-permute-start.2
Sparse Core Ops, SparseCore 0:
  17.7 550.7 all-gather.6
  754.9 536.3 all-gather.8
